TPU v7x, 512 devices: a whole 4x8x8 slice. The times are simulated.
512 devices in a mesh: section: 64 (over z, y_hi, core), tensor: 8 (over x, y_lo).
Axes of the slice: x: 4, y: 8 (y_hi: 4, y_lo: 2; y = y_hi * 2 + y_lo), z: 8, core: 2. Of those that a mesh axis runs over, the one named last changes fastest.
Arguments:
- grad_in: bfloat16 [64, 256, 6144], P('section', None, 'tensor'), may hold values from -6 to 6
- loss_grad: bfloat16 [256, 6144], P(None, 'tensor'), may hold values from -6 to 6
- queries: bfloat16 [64, 2, 256, 6144], P('section', None, None, 'tensor'), may hold values from -32 to 32
- attn_keys: bfloat16 [64, 2, 256, 6144], P('section', None, None, 'tensor'), may hold values from -32 to 32
- stored_input: bfloat16 [64, 2, 256, 6144], P('section', None, 'tensor'), may hold values from -6 to 6
- block_scales: bfloat16 [64, 2, 256, 48], P('section', None, 'tensor'), may hold values from 0.25 to 4
Outputs:
- grad_next: bfloat16 [64, 256, 6144], P('section', None, 'tensor')
- query_grad: bfloat16 [64, 2, 256, 6144], P('section', None, None, 'tensor')
- key_grad: bfloat16 [64, 2, 256, 6144], P('section', None, None, 'tensor')
All inputs are finite; a program needn't handle non-finite values.
Results may differ from a plain program's by a relative error of at most 0.0063.
Values may be sent and summed in bfloat16 or wider, within the bound.
A program may use at most 64 MiB of HBM per device.

v0:
```python
import math
import jax
import jax.numpy as jnp
from jax import lax
from jax.sharding import PartitionSpec as P

HD = 128


def passed_along(value, axis, steps):
    count = lax.axis_size(axis)
    leading, last = (max(0, -steps), min(count, count - steps))
    return lax.ppermute(value, axis, [(source, source + steps) for source in range(leading, last)])


def to_heads(flat):
    tokens, width = flat.shape
    return flat.reshape(tokens, width // HD, HD).transpose(1, 0, 2)


def from_heads(split):
    heads, tokens, depth = split.shape
    return split.transpose(1, 0, 2).reshape(tokens, heads * depth)


def attention_weights(query_heads, key_heads):
    tokens = query_heads.shape[1]
    scores = jnp.einsum(
        "htd,hjd->htj", query_heads, key_heads, preferred_element_type=jnp.float32
    ) * (1.0 / math.sqrt(HD))
    causal = lax.broadcasted_iota(jnp.int32, (tokens, tokens), 0) >= lax.broadcasted_iota(
        jnp.int32, (tokens, tokens), 1
    )
    scores = jnp.where(causal[None], scores, -1e30)
    scores = scores - jnp.max(scores, axis=-1, keepdims=True)
    expon = jnp.exp(scores)
    return expon / jnp.sum(expon, axis=-1, keepdims=True)


def value_grad(weights, upstream, upstream_heads):
    rounded = weights.astype(jnp.bfloat16)
    carried = jnp.einsum(
        "htj,htd->hjd", rounded, upstream_heads, preferred_element_type=jnp.float32
    )
    return (upstream.astype(jnp.float32) + from_heads(carried)).astype(jnp.bfloat16)


def score_grads(weights, upstream_heads, input_heads, query_heads, key_heads):
    product = jnp.einsum(
        "htd,hjd->htj", upstream_heads, input_heads, preferred_element_type=jnp.float32
    )
    centre = jnp.sum(weights * product, axis=-1, keepdims=True)
    score_diff = (weights * (product - centre)).astype(jnp.bfloat16)
    scaling = 1.0 / math.sqrt(HD)
    query_out = (
        jnp.einsum("htj,hjd->htd", score_diff, key_heads, preferred_element_type=jnp.float32)
        * scaling
    ).astype(jnp.bfloat16)
    key_out = (
        jnp.einsum("htj,htd->hjd", score_diff, query_heads, preferred_element_type=jnp.float32)
        * scaling
    ).astype(jnp.bfloat16)
    return (from_heads(query_out), from_heads(key_out))


def dequantize(values, scales):
    value_heads = to_heads(values).astype(jnp.float32)
    scale_heads = scales.astype(jnp.float32).T[:, :, None]
    return (value_heads * scale_heads).astype(jnp.bfloat16)


def local(grad_in, loss_grad, queries, attn_keys, stored_input, block_scales):
    grad_first = grad_in[0]
    query_pair = queries[0]
    key_pair = attn_keys[0]
    is_last = lax.axis_index("section") == lax.axis_size("section") - 1
    query_first_heads = to_heads(query_pair[0])
    key_first_heads = to_heads(key_pair[0])
    grad_first_heads = to_heads(grad_first)
    weights_first = attention_weights(query_first_heads, key_first_heads)
    input_first = value_grad(weights_first, grad_first, grad_first_heads)
    received = passed_along(input_first, "section", -1)
    grad_second = jnp.where(is_last, loss_grad, received)
    grad_second_heads = to_heads(grad_second)
    query_second_heads = to_heads(query_pair[1])
    key_second_heads = to_heads(key_pair[1])
    weights_second = attention_weights(query_second_heads, key_second_heads)
    input_second = value_grad(weights_second, grad_second, grad_second_heads)
    columns, column_scales = (
        lax.all_to_all(stored_input[0], "tensor", split_axis=2, concat_axis=1, tiled=True),
        lax.all_to_all(block_scales[0], "tensor", split_axis=2, concat_axis=1, tiled=True),
    )
    inputs_first = dequantize(columns[0], column_scales[0])
    inputs_second = dequantize(columns[1], column_scales[1])
    query_first, key_first = score_grads(
        weights_first, grad_first_heads, inputs_first, query_first_heads, key_first_heads
    )
    query_second, key_second = score_grads(
        weights_second, grad_second_heads, inputs_second, query_second_heads, key_second_heads
    )
    grad_next = passed_along(input_second, "section", -1)
    query_grad = jnp.stack([query_first, query_second])
    key_grad = jnp.stack([key_first, key_second])
    return (grad_next[None], query_grad[None], key_grad[None])


def solution(mesh):
    return jax.shard_map(
        local,
        mesh=mesh,
        in_specs=(
            P("section", None, "tensor"),
            P(None, "tensor"),
            P("section", None, None, "tensor"),
            P("section", None, None, "tensor"),
            P("section", None, "tensor", None),
            P("section", None, "tensor", None),
        ),
        out_specs=(
            P("section", None, "tensor"),
            P("section", None, None, "tensor"),
            P("section", None, None, "tensor"),
        ),
        check_vma=False,
    )
```

profile of v0, /device:TPU:249, one launch (start us, length us, event | category | flops | bytes accessed | tf_op | source)
XLA Modules:
  0.0 87.2 jit_solution(11047999192089381704)
XLA Ops:
  0.6 0.6 iota_compare_fusion
  1.3 2.0 %fusion.51 = (bf16[1,1,256,768]{3,2,1,0:T(8,128)(2,1)}, bf16[1,1,256,768]{3,2,1,0:T(8,128)(2,1)S(1)}) fusion(bf16[1,2,256,768]{3,2,1,0:T(8,128)(2,1)} %param.8), kind=kLoop, calls=%fused_computation.60 | loop fusion | bytes 1572864 | tf_op jit(solution)/shard_map/slice | solution.py:85
  3.7 0.8 fusion.52
  5.1 1.6 %fusion.53 = (f32[6,256]{1,0:T(8,128)S(1)}, f32[6,256,256]{1,2,0:T(8,128)S(1)}) fusion(pred[256,256]{0,1:T(8,128)(4,1)} %iota_compare_fusion, bf16[256,6,128]{2,0,1:T(8,128)(2,1)S(1)} %copy.106, bf16[256,6,128]{2,0,1:T(8,128)(2,1)S(1)} %copy.104), kind=kOutput, calls=%fused_computation.62 | convolution fusion | flops 102236416 | bytes 2430976 | tf_op jit(solution)/shard_map/sub | solution.py:35
  6.7 0.4 fusion.19
  7.1 0.7 copy-done.7
  7.8 0.8 fusion.16
  8.7 2.6 %collective-permute-start = (bf16[256,768]{0,1:T(8,128)(2,1)}, bf16[256,768]{0,1:T(8,128)(2,1)}, u32[]{:S(2)}, u32[]{:S(2)}) collective-permute-start(bf16[256,768]{0,1:T(8,128)(2,1)} %fusion.16), channel_id=1, source_target_pairs={{8,0},{16,8},{24,16},{32,24},{40,32},{48,40},{56,48},{64,56},{72,6... | collective-permute-start | bytes 1179656 | tf_op jit(solution)/shard_map/ppermute | solution.py:13
  11.4 0.7 reshape.66
  12.1 5.2 %all-to-all-start.1 = ((bf16[8,2,192]{2,1,0:T(2,128)(2,1)}), bf16[8,2,192]{2,1,0:T(2,128)(2,1)S(1)}, u32[]{:S(2)}, u32[]{:S(2)}) async-start(bf16[8,2,192]{2,1,0:T(2,128)(2,1)} %reshape.66), calls=%async_computation.1 | async-start | bytes 16384 | tf_op jit(solution)/shard_map/all_to_all | solution.py:91
  17.3 5.1 %copy.115 = bf16[1,2,32,6144]{2,1,3,0:T(2,128)(2,1)} copy(bf16[1,2,32,6144]{3,2,1,0:T(8,128)(2,1)S(1)} %copy-done.14) | data formatting | bytes 1572864 | tf_op args[4]
  22.4 4.7 %bitcast_bitcast_fusion = bf16[6144,2,32]{2,1,0:T(2,128)(2,1)S(1)} fusion(bf16[1,2,32,6144]{2,1,3,0:T(2,128)(2,1)} %copy.115), kind=kLoop, calls=%fused_computation.64 | loop fusion | bytes 1572864
  27.1 1.9 %copy.109 = bf16[256,768]{0,1:T(8,128)(2,1)} copy(bf16[256,768]{1,0:T(8,128)(2,1)} %param.7) | data formatting | bytes 786432 | tf_op args[1]
  29.0 1.9 %copy.160 = bf16[1,1,256,768]{2,3,1,0:T(8,128)(2,1)} copy(bf16[1,1,256,768]{3,2,1,0:T(8,128)(2,1)} %get-tuple-element.14) | data formatting | bytes 786432
  30.9 1.9 %copy.111 = bf16[256,6,128]{2,0,1:T(8,128)(2,1)} copy(bf16[256,6,128]{0,2,1:T(8,128)(2,1)} %bitcast.150) | data formatting | bytes 786432 | tf_op jit(solution)/shard_map/reshape;squeeze | solution.py:18
  32.8 1.9 %copy.161 = bf16[1,1,256,768]{2,3,1,0:T(8,128)(2,1)} copy(bf16[1,1,256,768]{3,2,1,0:T(8,128)(2,1)} %get-tuple-element.16) | data formatting | bytes 786432
  34.7 1.9 %copy.113 = bf16[256,6,128]{2,0,1:T(8,128)(2,1)} copy(bf16[256,6,128]{0,2,1:T(8,128)(2,1)} %bitcast.152) | data formatting | bytes 786432 | tf_op jit(solution)/shard_map/reshape;squeeze | solution.py:18
  36.7 3.7 %reshape.64 = bf16[8,2,24576]{2,1,0:T(2,128)(2,1)} reshape(bf16[6144,2,32]{2,1,0:T(2,128)(2,1)S(1)} %bitcast_bitcast_fusion) | data formatting | bytes 1572864
  40.3 5.3 %all-to-all-start = ((bf16[8,2,24576]{2,1,0:T(2,128)(2,1)}), bf16[8,2,24576]{2,1,0:T(2,128)(2,1)}, u32[]{:S(2)}, u32[]{:S(2)}) async-start(bf16[8,2,24576]{2,1,0:T(2,128)(2,1)} %reshape.64), calls=%async_computation | async-start | bytes 1572864 | tf_op jit(solution)/shard_map/all_to_all | solution.py:90
  45.7 0.6 fusion.58
  46.3 0.3 copy-done.6
  46.6 1.3 %broadcast_select_fusion = bf16[256,768]{0,1:T(8,128)(2,1)S(1)} fusion(bf16[256,768]{0,1:T(8,128)(2,1)S(1)} %copy-done.6, bf16[256,768]{0,1:T(8,128)(2,1)} %collective-permute-done, pred[]{:T(512)S(6)} %eq.3), kind=kLoop, calls=%fused_computation.49 | loop fusion | flops 196608 | bytes 1179649 | tf_op jit(solution)/shard_map/jit(_where)/select_n | solution.py:83
  47.9 0.4 fusion.17
  48.3 0.3 copy-done.11
  48.8 4.6 %collective-permute-start.1 = (bf16[256,768]{0,1:T(8,128)(2,1)S(1)}, bf16[256,768]{0,1:T(8,128)(2,1)S(1)}, u32[]{:S(2)}, u32[]{:S(2)}) collective-permute-start(bf16[256,768]{0,1:T(8,128)(2,1)S(1)} %fusion.15), channel_id=1, source_target_pairs={{8,0},{16,8},{24,16},{32,24},{40,32},{48,40},{56,48},{64,56},{72,6... | collective-permute-start | bytes 1179656 | tf_op jit(solution)/shard_map/ppermute | solution.py:13
  53.6 0.8 copy.124
  54.4 0.8 copy.119
  55.2 12.1 %collective-permute-done.1 = bf16[256,768]{0,1:T(8,128)(2,1)S(1)} collective-permute-done((bf16[256,768]{0,1:T(8,128)(2,1)S(1)}, bf16[256,768]{0,1:T(8,128)(2,1)S(1)}, u32[]{:S(2)}, u32[]{:S(2)}) %collective-permute-start.1) | collective-permute-done | bytes 393248 | tf_op jit(solution)/shard_map/ppermute | solution.py:13
  67.3 0.9 %copy.137 = bf16[1,256,768]{2,1,0:T(8,128)(2,1)} copy(bf16[1,256,768]{1,2,0:T(8,128)(2,1)S(1)} %bitcast.163) | data formatting | bytes 786432
  68.2 3.2 %reshape.65 = bf16[6144,2,32]{2,1,0:T(2,128)(2,1)S(1)} reshape(bf16[8,2,24576]{2,1,0:T(2,128)(2,1)} %all-to-all-done) | data formatting | bytes 1572864
  71.4 4.9 %copy.116 = bf16[2,32,8,768]{3,1,2,0:T(8,128)(2,1)} copy(bf16[2,32,8,768]{1,0,3,2:T(2,128)(2,1)S(1)} %bitcast.145) | data formatting | bytes 1572864 | tf_op jit(solution)/shard_map/all_to_all | solution.py:90
  76.4 1.3 %slice_convert_fusion.1 = (f32[1,8,32,768]{3,2,1,0:T(8,128)S(1)}, f32[1,8,32,768]{3,2,1,0:T(8,128)S(1)}) fusion(bf16[2,8,32,768]{3,2,1,0:T(8,128)(2,1)} %bitcast.154), kind=kLoop, calls=%fused_computation.40 | loop fusion | flops 393216 | bytes 2359296 | tf_op jit(solution)/shard_map/convert_element_type | solution.py:67
  77.8 0.3 fusion.13
  78.2 0.5 copy-done.12
  78.7 0.6 copy-done.10
  79.3 0.4 multiply_reduce_fusion
  79.7 0.3 multiply_convert_fusion
  80.0 0.7 copy-done.2
  80.6 0.4 fusion.10
  81.2 0.3 fusion.12
  81.8 0.6 copy-done.15
  82.4 0.3 fusion.14
  82.8 1.1 %copy-done.8 = f32[6,256,256]{1,2,0:T(8,128)S(1)} copy-done((f32[6,256,256]{1,2,0:T(8,128)S(1)}, f32[6,256,256]{1,2,0:T(8,128)}, u32[]{:S(2)}) %copy-start.8) | copy-done | bytes 1572888
  83.9 0.4 fusion.4
  84.2 0.3 fusion.6
  84.5 0.4 fusion.9
  85.1 0.4 copy-done.1
  86.0 1.3 %maximum_bitcast_fusion = (bf16[1,2,256,768]{3,2,1,0:T(8,128)(2,1)}, bf16[1,2,256,768]{3,2,1,0:T(8,128)(2,1)}) fusion(bf16[1,256,768]{2,1,0:T(8,128)(2,1)S(1)} %copy.130, bf16[1,256,768]{2,1,0:T(8,128)(2,1)S(1)} %copy.129, bf16[1,256,768]{2,1,0:T(8,128)(2,1)S(1)} %copy.136, bf16[1,256,768]{2,1,0:T(8,128)(2,1)S(1)} %copy.135), kind=kLoop, calls=%fused_computation.27 | loop fusion | flops 786432 | bytes 3145728 | tf_op jit(solution)/shard_map/broadcast_in_dim | solution.py:104
  (62 shorter events, 2.7 us)
Async XLA Ops:
  1.3 2.4 %copy-start.13 = (bf16[1,2,256,768]{3,2,1,0:T(8,128)(2,1)S(1)}, bf16[1,2,256,768]{3,2,1,0:T(8,128)(2,1)}, u32[]{:S(2)}) copy-start(bf16[1,2,256,768]{3,2,1,0:T(8,128)(2,1)} %param.9) | copy-start | bytes 2359300
  3.7 1.2 %copy-start.17 = (bf16[1,256,768]{2,1,0:T(8,128)(2,1)S(1)}, bf16[1,256,768]{2,1,0:T(8,128)(2,1)}, u32[]{:S(2)}) copy-start(bf16[1,256,768]{2,1,0:T(8,128)(2,1)} %param.6) | copy-start | bytes 1179652
  4.7 2.0 %copy-start = (bf16[1,1,256,768]{2,3,1,0:T(8,128)(2,1)}, bf16[1,1,256,768]{2,3,1,0:T(8,128)(2,1)S(1)}, u32[]{:S(2)}) copy-start(bf16[1,1,256,768]{2,3,1,0:T(8,128)(2,1)S(1)} %copy.159) | copy-start | bytes 1179652
  5.1 2.0 %copy-start.4 = (bf16[1,256,768]{1,2,0:T(8,128)(2,1)}, bf16[1,256,768]{1,2,0:T(8,128)(2,1)S(1)}, u32[]{:S(2)}) copy-start(bf16[1,256,768]{1,2,0:T(8,128)(2,1)S(1)} %copy.102) | copy-start | bytes 1179652
  6.7 1.2 %copy-start.7 = (f32[6,256,256]{1,2,0:T(8,128)}, f32[6,256,256]{1,2,0:T(8,128)S(1)}, u32[]{:S(2)}) copy-start(f32[6,256,256]{1,2,0:T(8,128)S(1)} %get-tuple-element.21) | copy-start | bytes 4718596
  7.8 3.4 %copy-start.21 = (bf16[1,2,32,48]{3,2,1,0:T(8,128)(2,1)S(1)}, bf16[1,2,32,48]{3,2,1,0:T(8,128)(2,1)}, u32[]{:S(2)}) copy-start(bf16[1,2,32,48]{3,2,1,0:T(8,128)(2,1)} %param.11) | copy-start | bytes 18436
  7.8 9.4 %copy-start.14 = (bf16[1,2,32,6144]{3,2,1,0:T(8,128)(2,1)S(1)}, bf16[1,2,32,6144]{3,2,1,0:T(8,128)(2,1)}, u32[]{:S(2)}) copy-start(bf16[1,2,32,6144]{3,2,1,0:T(8,128)(2,1)} %param.10) | copy-start | bytes 2359300
  8.7 37.7 %collective-permute-start = (bf16[256,768]{0,1:T(8,128)(2,1)}, bf16[256,768]{0,1:T(8,128)(2,1)}, u32[]{:S(2)}, u32[]{:S(2)}) collective-permute-start(bf16[256,768]{0,1:T(8,128)(2,1)} %fusion.16), channel_id=1, source_target_pairs={{8,0},{16,8},{24,16},{32,24},{40,32},{48,40},{56,48},{64,56},{72,6... | collective-permute-start | bytes 1179656 | tf_op jit(solution)/shard_map/ppermute | solution.py:13
  12.1 28.3 %all-to-all-start.1 = ((bf16[8,2,192]{2,1,0:T(2,128)(2,1)}), bf16[8,2,192]{2,1,0:T(2,128)(2,1)S(1)}, u32[]{:S(2)}, u32[]{:S(2)}) async-start(bf16[8,2,192]{2,1,0:T(2,128)(2,1)} %reshape.66), calls=%async_computation.1 | async-start | bytes 16384 | tf_op jit(solution)/shard_map/all_to_all | solution.py:91
  40.3 5.3 %copy-start.18 = (bf16[256,6,128]{2,0,1:T(8,128)(2,1)S(1)}, bf16[256,6,128]{2,0,1:T(8,128)(2,1)}, u32[]{:S(2)}) copy-start(bf16[256,6,128]{2,0,1:T(8,128)(2,1)} %copy.111) | copy-start | bytes 1179652
  40.3 5.3 %copy-start.19 = (bf16[256,6,128]{2,0,1:T(8,128)(2,1)S(1)}, bf16[256,6,128]{2,0,1:T(8,128)(2,1)}, u32[]{:S(2)}) copy-start(bf16[256,6,128]{2,0,1:T(8,128)(2,1)} %copy.113) | copy-start | bytes 1179652
  40.3 5.3 %copy-start.20 = (pred[256,256]{0,1:T(8,128)(4,1)S(1)}, pred[256,256]{0,1:T(8,128)(4,1)}, u32[]{:S(2)}) copy-start(pred[256,256]{0,1:T(8,128)(4,1)} %iota_compare_fusion) | copy-start | bytes 196612
  40.3 27.9 %all-to-all-start = ((bf16[8,2,24576]{2,1,0:T(2,128)(2,1)}), bf16[8,2,24576]{2,1,0:T(2,128)(2,1)}, u32[]{:S(2)}, u32[]{:S(2)}) async-start(bf16[8,2,24576]{2,1,0:T(2,128)(2,1)} %reshape.64), calls=%async_computation | async-start | bytes 1572864 | tf_op jit(solution)/shard_map/all_to_all | solution.py:90
  45.6 1.0 %copy-start.6 = (bf16[256,768]{0,1:T(8,128)(2,1)S(1)}, bf16[256,768]{0,1:T(8,128)(2,1)}, u32[]{:S(2)}) copy-start(bf16[256,768]{0,1:T(8,128)(2,1)} %copy.109) | copy-start | bytes 1179652
  46.3 2.0 %copy-start.9 = (f32[6,256,256]{1,2,0:T(8,128)}, f32[6,256,256]{1,2,0:T(8,128)S(1)}, u32[]{:S(2)}) copy-start(f32[6,256,256]{1,2,0:T(8,128)S(1)} %get-tuple-element.23) | copy-start | bytes 4718596
  46.3 2.0 %copy-start.22 = (f32[6,256]{1,0:T(8,128)}, f32[6,256]{1,0:T(8,128)S(1)}, u32[]{:S(2)}) copy-start(f32[6,256]{1,0:T(8,128)S(1)} %get-tuple-element.22) | copy-start | bytes 18436
  47.9 0.8 copy-start.11
  48.8 18.5 %collective-permute-start.1 = (bf16[256,768]{0,1:T(8,128)(2,1)S(1)}, bf16[256,768]{0,1:T(8,128)(2,1)S(1)}, u32[]{:S(2)}, u32[]{:S(2)}) collective-permute-start(bf16[256,768]{0,1:T(8,128)(2,1)S(1)} %fusion.15), channel_id=1, source_target_pairs={{8,0},{16,8},{24,16},{32,24},{40,32},{48,40},{56,48},{64,56},{72,6... | collective-permute-start | bytes 1179656 | tf_op jit(solution)/shard_map/ppermute | solution.py:13
  76.4 1.5 %copy-start.16 = (f32[6,256]{0,1:T(8,128)S(1)}, f32[6,256]{0,1:T(8,128)}, u32[]{:S(2)}) copy-start(f32[6,256]{0,1:T(8,128)} %copy.124) | copy-start | bytes 18436
  77.7 1.0 %copy-start.12 = (bf16[256,768]{0,1:T(8,128)(2,1)S(1)}, bf16[256,768]{0,1:T(8,128)(2,1)}, u32[]{:S(2)}) copy-start(bf16[256,768]{0,1:T(8,128)(2,1)} %copy-done.11) | copy-start | bytes 1179652
  77.7 1.0 %copy-start.23 = (f32[6,256]{1,0:T(8,128)S(1)}, f32[6,256]{1,0:T(8,128)}, u32[]{:S(2)}) copy-start(f32[6,256]{1,0:T(8,128)} %copy-done.22) | copy-start | bytes 18436
  77.8 1.4 %copy-start.10 = (f32[6,256,256]{1,2,0:T(8,128)S(1)}, f32[6,256,256]{1,2,0:T(8,128)}, u32[]{:S(2)}) copy-start(f32[6,256,256]{1,2,0:T(8,128)} %copy-done.9) | copy-start | bytes 4718596
  79.6 1.0 %copy-start.2 = (bf16[1,1,256,768]{2,3,1,0:T(8,128)(2,1)S(1)}, bf16[1,1,256,768]{2,3,1,0:T(8,128)(2,1)}, u32[]{:S(2)}) copy-start(bf16[1,1,256,768]{2,3,1,0:T(8,128)(2,1)} %copy.160) | copy-start | bytes 1179652
  79.9 1.3 %copy-start.3 = (bf16[1,1,256,768]{2,3,1,0:T(8,128)(2,1)S(1)}, bf16[1,1,256,768]{2,3,1,0:T(8,128)(2,1)}, u32[]{:S(2)}) copy-start(bf16[1,1,256,768]{2,3,1,0:T(8,128)(2,1)} %copy.161) | copy-start | bytes 1179652
  81.5 0.9 %copy-start.15 = (f32[6,256]{0,1:T(8,128)S(1)}, f32[6,256]{0,1:T(8,128)}, u32[]{:S(2)}) copy-start(f32[6,256]{0,1:T(8,128)} %copy.119) | copy-start | bytes 18436
  81.7 1.1 %copy-start.5 = (bf16[1,256,768]{1,2,0:T(8,128)(2,1)S(1)}, bf16[1,256,768]{1,2,0:T(8,128)(2,1)}, u32[]{:S(2)}) copy-start(bf16[1,256,768]{1,2,0:T(8,128)(2,1)} %copy-done.4) | copy-start | bytes 1179652
  82.4 1.4 %copy-start.8 = (f32[6,256,256]{1,2,0:T(8,128)S(1)}, f32[6,256,256]{1,2,0:T(8,128)}, u32[]{:S(2)}) copy-start(f32[6,256,256]{1,2,0:T(8,128)} %copy-done.7) | copy-start | bytes 4718596
  84.5 1.0 %copy-start.1 = (bf16[1,1,256,768]{2,3,1,0:T(8,128)(2,1)S(1)}, bf16[1,1,256,768]{2,3,1,0:T(8,128)(2,1)}, u32[]{:S(2)}) copy-start(bf16[1,1,256,768]{2,3,1,0:T(8,128)(2,1)} %copy-done) | copy-start | bytes 1179652
where the time goes:
time: 88.1 us; the launch traced here: 87.2 us
  local copies, waits for them, and re-layouts  44.7 us (51%)
  starting transfers between devices  17.7 us (20%)
  waiting for transfers between devices  12.1 us (14%)
  other arithmetic  6.65 us (8%)
  matrix products  5.05 us (6%)
  between operations  1.09 us (1%)
    unnamed x63, local copies, waits for them, and re-layouts  30 us
    ppermute x2, waiting for transfers between devices, passed_along(): lax.ppermute(value, axis, [(source, source + steps) for source in range(l...  12.1 us
    ppermute x2, starting transfers between devices, passed_along(): lax.ppermute(value, axis, [(source, source + steps) for source in range(l...  7.17 us
    all_to_all x1, starting transfers between devices, local(): lax.all_to_all(stored_input[0], 'tensor', split_axis=2, concat_axis=1, ti...  5.29 us
    all_to_all x1, starting transfers between devices, local(): lax.all_to_all(block_scales[0], 'tensor', split_axis=2, concat_axis=1, ti...  5.2 us
    all_to_all x1, local copies, waits for them, and re-layouts, local(): lax.all_to_all(stored_input[0], 'tensor', split_axis=2, concat_axis=1, ti...  4.92 us
    another operation x4, local copies, waits for them, and re-layouts, to_heads(): return flat.reshape(tokens, width // HD, HD).transpose(1, 0, 2)  4.28 us
    sub x2, matrix products, attention_weights(): scores = scores - jnp.max(scores, axis=-1, keepdims=True)  2.21 us
  transfers between devices with their start and end apart: 4, of which 1 were waited for; matrix products, arithmetic and copies ran while one was open for 33% of the time, Pallas kernels for 0%

commit v1 on v0

--- a/solution.py
+++ b/solution.py
@@ -3,8 +3,18 @@
 import jax.numpy as jnp
 from jax import lax
 from jax.sharding import PartitionSpec as P
+from jax.lax import all_to_all, axis_size
 
 HD = 128
+post_the_rates = lambda local_block, along_axis, join_dim, at_axis: jnp.concatenate(
+    all_to_all(
+        jnp.stack(jnp.split(local_block, axis_size(along_axis), join_dim), 0),
+        axis_name=along_axis,
+        split_axis=0,
+        concat_axis=0,
+    ),
+    at_axis,
+)
 
 
 def passed_along(value, axis, steps):
@@ -87,7 +97,7 @@
     weights_second = attention_weights(query_second_heads, key_second_heads)
     input_second = value_grad(weights_second, grad_second, grad_second_heads)
     columns, column_scales = (
-        lax.all_to_all(stored_input[0], "tensor", split_axis=2, concat_axis=1, tiled=True),
+        post_the_rates(stored_input[0], "tensor", 2, at_axis=1),
         lax.all_to_all(block_scales[0], "tensor", split_axis=2, concat_axis=1, tiled=True),
     )
     inputs_first = dequantize(columns[0], column_scales[0])

time: 88.1 us -> 68.6 us (0.78)
  the two profiles are of different devices: /device:TPU:249 before, /device:TPU:1 now
where the time goes in v1:
time: 68.6 us; the launch traced here: 67.9 us
  starting transfers between devices  19.5 us (28%)
  local copies, waits for them, and re-layouts  19.2 us (28%)
  matrix products  11.1 us (16%)
  waiting for transfers between devices  11.1 us (16%)
  other arithmetic  6.16 us (9%)
  between operations  0.98 us (1%)
    ppermute x2, waiting for transfers between devices, passed_along(): lax.ppermute(value, axis, [(source, source + steps) for source in range(l...  11.1 us
    unnamed x48, local copies, waits for them, and re-layouts  10.3 us
    ppermute x2, starting transfers between devices, passed_along(): lax.ppermute(value, axis, [(source, source + steps) for source in range(l...  8.24 us
    all_to_all x1, starting transfers between devices, local(): lax.all_to_all(block_scales[0], 'tensor', split_axis=2, concat_axis=1, ti...  5.86 us
    all_to_all x1, starting transfers between devices, all_to_all(jnp.stack(jnp.split(local_block, axis_size(along_axis), join_d...  5.36 us
    sub x2, matrix products, attention_weights(): scores = scores - jnp.max(scores, axis=-1, keepdims=True)  5.13 us
    dot_general x2, matrix products, value_grad(): jnp.einsum('htj,htd->hjd', rounded, upstream_heads, preferred_element_typ...  2.36 us
    another operation x4, local copies, waits for them, and re-layouts, to_heads(): return flat.reshape(tokens, width // HD, HD).transpose(1, 0, 2)  2.28 us
  transfers between devices with their start and end apart: 4, of which 1 were waited for; matrix products, arithmetic and copies ran while one was open for 32% of the time, Pallas kernels for 0%

profile of v1, /device:TPU:1, one launch (start us, length us, event | category | flops | bytes accessed | tf_op | source)
XLA Modules:
  0.0 67.9 jit_solution(8091195314730275101)
XLA Ops:
  0.6 0.8 %copy.114 = bf16[1,2,32,48]{2,1,3,0:T(2,128)(2,1)S(1)} copy(bf16[1,2,32,48]{3,2,1,0:T(8,128)(2,1)} %param.11) | data formatting | bytes 12288 | tf_op args[5]
  1.5 0.7 %reshape.69 = bf16[8,2,192]{2,1,0:T(2,128)(2,1)} reshape(bf16[48,2,32]{2,1,0:T(2,128)(2,1)S(1)} %bitcast_bitcast_fusion) | data formatting | bytes 12288
  2.2 5.9 %all-to-all-start.1 = ((bf16[8,2,192]{2,1,0:T(2,128)(2,1)}), bf16[8,2,192]{2,1,0:T(2,128)(2,1)S(1)}, u32[]{:S(2)}, u32[]{:S(2)}) async-start(bf16[8,2,192]{2,1,0:T(2,128)(2,1)} %reshape.69), calls=%async_computation.1 | async-start | bytes 16384 | tf_op jit(solution)/shard_map/all_to_all | solution.py:101
  8.0 0.7 iota_compare_fusion
  8.7 1.2 %fusion.59 = (bf16[1,1,256,768]{3,2,1,0:T(8,128)(2,1)S(1)}, bf16[1,1,256,768]{3,2,1,0:T(8,128)(2,1)S(1)}) fusion(bf16[1,2,256,768]{3,2,1,0:T(8,128)(2,1)} %param.8), kind=kLoop, calls=%fused_computation.76 | loop fusion | bytes 1572864 | tf_op jit(solution)/shard_map/slice | solution.py:95
  10.1 0.9 %copy.103 = bf16[256,6,128]{2,0,1:T(8,128)(2,1)} copy(bf16[256,6,128]{0,2,1:T(8,128)(2,1)S(1)} %bitcast.176) | data formatting | bytes 786432 | tf_op jit(solution)/shard_map/reshape;squeeze | solution.py:28
  11.2 0.9 %copy.105 = bf16[256,6,128]{2,0,1:T(8,128)(2,1)} copy(bf16[256,6,128]{0,2,1:T(8,128)(2,1)S(1)} %bitcast.178) | data formatting | bytes 786432 | tf_op jit(solution)/shard_map/reshape;squeeze | solution.py:28
  12.3 1.9 %fusion.61 = (f32[6,256]{1,0:T(8,128)S(1)}, f32[6,256,256]{1,2,0:T(8,128)S(1)}) fusion(pred[256,256]{0,1:T(8,128)(4,1)} %iota_compare_fusion, bf16[256,6,128]{2,0,1:T(8,128)(2,1)} %copy.105, bf16[256,6,128]{2,0,1:T(8,128)(2,1)} %copy.103), kind=kOutput, calls=%fused_computation.78 | convolution fusion | flops 102236416 | bytes 2430976 | tf_op jit(solution)/shard_map/sub | solution.py:45
  14.3 0.4 fusion.19
  14.7 0.8 %fusion.16 = bf16[256,768]{0,1:T(8,128)(2,1)} fusion(f32[6,256,128]{1,2,0:T(8,128)S(1)} %fusion.19, bf16[1,256,768]{1,2,0:T(8,128)(2,1)S(1)} %copy.101), kind=kLoop, calls=%fused_computation.32 | loop fusion | flops 589824 | bytes 1572864 | tf_op jit(solution)/shard_map/convert_element_type | solution.py:55
  15.5 6.3 %collective-permute-start = (bf16[256,768]{0,1:T(8,128)(2,1)}, bf16[256,768]{0,1:T(8,128)(2,1)}, u32[]{:S(2)}, u32[]{:S(2)}) collective-permute-start(bf16[256,768]{0,1:T(8,128)(2,1)} %fusion.16), channel_id=1, source_target_pairs={{8,0},{16,8},{24,16},{32,24},{40,32},{48,40},{56,48},{64,56},{72,6... | collective-permute-start | bytes 1179656 | tf_op jit(solution)/shard_map/ppermute | solution.py:23
  21.9 0.6 fusion.36
  22.5 0.6 fusion.35
  23.2 0.6 fusion.34
  23.8 0.6 fusion.33
  24.5 0.6 fusion.32
  25.1 0.6 fusion.31
  25.8 0.6 fusion.30
  26.4 0.6 fusion.29
  27.4 0.2 copy.110
  27.8 0.2 copy.112
  28.1 5.4 %all-to-all-start = ((bf16[8,2,32,768]{3,2,1,0:T(8,128)(2,1)}), bf16[8,2,32,768]{3,2,1,0:T(8,128)(2,1)S(1)}, u32[]{:S(2)}, u32[]{:S(2)}) async-start(bf16[8,2,32,768]{3,2,1,0:T(8,128)(2,1)} %fusion.29), calls=%async_computation | async-start | bytes 1572864 | tf_op jit(solution)/shard_map/all_to_all | solution.py:10
  33.4 3.2 %fusion.66 = (f32[6,256]{1,0:T(8,128)}, f32[6,256,256]{1,2,0:T(8,128)}) fusion(pred[256,256]{0,1:T(8,128)(4,1)} %iota_compare_fusion, bf16[256,6,128]{2,0,1:T(8,128)(2,1)S(1)} %copy.112, bf16[256,6,128]{2,0,1:T(8,128)(2,1)S(1)} %copy.110), kind=kOutput, calls=%fused_computation.79 | convolution fusion | flops 102236416 | bytes 2430976 | tf_op jit(solution)/shard_map/sub | solution.py:45
  36.7 1.0 %broadcast_select_fusion = bf16[256,768]{0,1:T(8,128)(2,1)S(1)} fusion(bf16[256,768]{0,1:T(8,128)(2,1)S(1)} %copy.108, bf16[256,768]{0,1:T(8,128)(2,1)} %collective-permute-done, pred[]{:T(512)S(6)} %eq.3), kind=kLoop, calls=%fused_computation.49 | loop fusion | flops 196608 | bytes 1179649 | tf_op jit(solution)/shard_map/jit(_where)/select_n | solution.py:93
  37.7 2.0 %fusion.17 = f32[6,256,128]{1,2,0:T(8,128)S(1)} fusion(bf16[6,256,128]{1,2,0:T(8,128)(2,1)S(1)} %bitcast.191, f32[6,256,256]{1,2,0:T(8,128)} %get-tuple-element.23, f32[6,256]{1,0:T(8,128)} %get-tuple-element.22), kind=kOutput, calls=%fused_computation.33 | convolution fusion | flops 101449728 | bytes 2758656 | tf_op jit(solution)/shard_map/htj,htd->hjd/dot_general | solution.py:52
  39.8 1.9 %collective-permute-start.1 = (bf16[256,768]{0,1:T(8,128)(2,1)S(1)}, bf16[256,768]{0,1:T(8,128)(2,1)S(1)}, u32[]{:S(2)}, u32[]{:S(2)}) collective-permute-start(bf16[256,768]{0,1:T(8,128)(2,1)S(1)} %fusion.15), channel_id=1, source_target_pairs={{8,0},{16,8},{24,16},{32,24},{40,32},{48,40},{56,48},{64,56},{72,6... | collective-permute-start | bytes 1179656 | tf_op jit(solution)/shard_map/ppermute | solution.py:23
  42.1 0.8 %copy.121 = f32[6,256]{0,1:T(8,128)} copy(f32[6,256]{1,0:T(8,128)S(1)} %bitcast.205) | data formatting | bytes 12288 | tf_op jit(solution)/shard_map/transpose | solution.py:78
  42.9 11.1 %collective-permute-done.1 = bf16[256,768]{0,1:T(8,128)(2,1)S(1)} collective-permute-done((bf16[256,768]{0,1:T(8,128)(2,1)S(1)}, bf16[256,768]{0,1:T(8,128)(2,1)S(1)}, u32[]{:S(2)}, u32[]{:S(2)}) %collective-permute-start.1) | collective-permute-done | bytes 393248 | tf_op jit(solution)/shard_map/ppermute | solution.py:23
  54.0 0.9 %copy.134 = bf16[1,256,768]{2,1,0:T(8,128)(2,1)} copy(bf16[1,256,768]{1,2,0:T(8,128)(2,1)S(1)} %bitcast.201) | data formatting | bytes 786432
  54.9 1.0 %slice_convert_fusion.1 = (f32[1,8,32,768]{3,2,0,1:T(8,128)}, f32[1,8,32,768]{3,2,0,1:T(8,128)S(1)}) fusion(bf16[2,8,32,768]{3,2,0,1:T(8,128)(2,1)S(1)} %bitcast.184), kind=kLoop, calls=%fused_computation.40 | loop fusion | flops 393216 | bytes 2359296 | tf_op jit(solution)/shard_map/convert_element_type | solution.py:77
  55.9 1.3 %reshape.65 = f32[256,6,128]{2,1,0:T(8,128)S(1)} reshape(f32[1,8,32,768]{3,2,0,1:T(8,128)} %get-tuple-element.12) | data formatting | bytes 1572864 | tf_op jit(solution)/shard_map/convert_element_type | solution.py:77
  57.2 0.3 fusion.14
  57.5 0.6 copy-done.3
  58.2 1.9 %fusion.4 = (f32[6,256]{1,0:T(8,128)S(1)}, f32[6,256,256]{2,1,0:T(8,128)S(1)}) fusion(f32[6,256,256]{1,2,0:T(8,128)} %copy-done.4, f32[6,256]{1,0:T(8,128)S(1)} %get-tuple-element.20, bf16[6,256,128]{1,2,0:T(8,128)(2,1)S(1)} %bitcast.186, bf16[6,256,128]{2,0,1:T(8,128)(2,1)S(1)} %fusion.14), kind=kOutput, calls=%fused_computation.6 | convolution fusion | flops 101841408 | bytes 3944448 | tf_op jit(solution)/shard_map/htd,hjd->htj/dot_general | solution.py:59
  60.1 0.3 fusion.6
  60.4 0.4 fusion.9
  60.8 0.9 %copy.132 = bf16[1,256,768]{2,1,0:T(8,128)(2,1)} copy(bf16[1,256,768]{1,2,0:T(8,128)(2,1)S(1)} %bitcast.189) | data formatting | bytes 786432 | tf_op jit(solution)/shard_map/stack;reshape | solution.py:113
  61.7 0.3 fusion.11
  62.0 0.9 %copy.126 = bf16[1,256,768]{2,1,0:T(8,128)(2,1)} copy(bf16[1,256,768]{1,2,0:T(8,128)(2,1)S(1)} %bitcast.187) | data formatting | bytes 786432 | tf_op jit(solution)/shard_map/stack;reshape | solution.py:112
  63.0 0.3 fusion.13
  63.4 0.5 copy-done.8
  63.9 0.6 copy-done.6
  64.5 0.4 multiply_reduce_fusion
  64.8 0.3 multiply_convert_fusion
  65.1 0.4 fusion.10
  65.7 0.3 fusion.12
  66.2 0.3 copy-done
  66.6 1.3 %maximum_bitcast_fusion = (bf16[1,2,256,768]{3,2,1,0:T(8,128)(2,1)}, bf16[1,2,256,768]{3,2,1,0:T(8,128)(2,1)}) fusion(bf16[1,256,768]{2,1,0:T(8,128)(2,1)S(1)} %copy.127, bf16[1,256,768]{2,1,0:T(8,128)(2,1)S(1)} %copy-done.1, bf16[1,256,768]{2,1,0:T(8,128)(2,1)S(1)} %copy.133, bf16[1,256,768]{2,1,0:T(8,128)(2,1)S(1)} %copy-done), kind=kLoop, calls=%fused_computation.27 | loop fusion | flops 786432 | bytes 3145728 | tf_op jit(solution)/shard_map/broadcast_in_dim | solution.py:114
  (47 shorter events, 2.2 us)
Async XLA Ops:
  2.2 25.9 %all-to-all-start.1 = ((bf16[8,2,192]{2,1,0:T(2,128)(2,1)}), bf16[8,2,192]{2,1,0:T(2,128)(2,1)S(1)}, u32[]{:S(2)}, u32[]{:S(2)}) async-start(bf16[8,2,192]{2,1,0:T(2,128)(2,1)} %reshape.69), calls=%async_computation.1 | async-start | bytes 16384 | tf_op jit(solution)/shard_map/all_to_all | solution.py:101
  8.7 2.3 %copy-start.10 = (bf16[1,2,256,768]{3,2,1,0:T(8,128)(2,1)S(1)}, bf16[1,2,256,768]{3,2,1,0:T(8,128)(2,1)}, u32[]{:S(2)}) copy-start(bf16[1,2,256,768]{3,2,1,0:T(8,128)(2,1)} %param.9) | copy-start | bytes 2359300
  11.0 1.2 %copy-start.12 = (bf16[1,256,768]{2,1,0:T(8,128)(2,1)S(1)}, bf16[1,256,768]{2,1,0:T(8,128)(2,1)}, u32[]{:S(2)}) copy-start(bf16[1,256,768]{2,1,0:T(8,128)(2,1)} %param.6) | copy-start | bytes 1179652
  12.3 2.3 %copy-start.2 = (bf16[1,256,768]{1,2,0:T(8,128)(2,1)}, bf16[1,256,768]{1,2,0:T(8,128)(2,1)S(1)}, u32[]{:S(2)}) copy-start(bf16[1,256,768]{1,2,0:T(8,128)(2,1)S(1)} %copy.101) | copy-start | bytes 1179652
  14.3 12.8 %copy-start.4 = (f32[6,256,256]{1,2,0:T(8,128)}, f32[6,256,256]{1,2,0:T(8,128)S(1)}, u32[]{:S(2)}) copy-start(f32[6,256,256]{1,2,0:T(8,128)S(1)} %get-tuple-element.21) | copy-start | bytes 4718596
  14.7 7.2 %copy-start.9 = (bf16[1,2,32,6144]{3,2,1,0:T(8,128)(2,1)S(1)}, bf16[1,2,32,6144]{3,2,1,0:T(8,128)(2,1)}, u32[]{:S(2)}) copy-start(bf16[1,2,32,6144]{3,2,1,0:T(8,128)(2,1)} %param.10) | copy-start | bytes 2359300
  15.5 11.5 %copy-start.13 = (bf16[256,768]{1,0:T(8,128)(2,1)S(1)}, bf16[256,768]{1,0:T(8,128)(2,1)}, u32[]{:S(2)}) copy-start(bf16[256,768]{1,0:T(8,128)(2,1)} %param.7) | copy-start | bytes 1179652
  15.5 21.1 %collective-permute-start = (bf16[256,768]{0,1:T(8,128)(2,1)}, bf16[256,768]{0,1:T(8,128)(2,1)}, u32[]{:S(2)}, u32[]{:S(2)}) collective-permute-start(bf16[256,768]{0,1:T(8,128)(2,1)} %fusion.16), channel_id=1, source_target_pairs={{8,0},{16,8},{24,16},{32,24},{40,32},{48,40},{56,48},{64,56},{72,6... | collective-permute-start | bytes 1179656 | tf_op jit(solution)/shard_map/ppermute | solution.py:23
  28.1 26.8 %all-to-all-start = ((bf16[8,2,32,768]{3,2,1,0:T(8,128)(2,1)}), bf16[8,2,32,768]{3,2,1,0:T(8,128)(2,1)S(1)}, u32[]{:S(2)}, u32[]{:S(2)}) async-start(bf16[8,2,32,768]{3,2,1,0:T(8,128)(2,1)} %fusion.29), calls=%async_computation | async-start | bytes 1572864 | tf_op jit(solution)/shard_map/all_to_all | solution.py:10
  37.7 2.0 %copy-start.7 = (bf16[256,768]{0,1:T(8,128)(2,1)}, bf16[256,768]{0,1:T(8,128)(2,1)S(1)}, u32[]{:S(2)}) copy-start(bf16[256,768]{0,1:T(8,128)(2,1)S(1)} %broadcast_select_fusion) | copy-start | bytes 1179652
  39.8 14.2 %collective-permute-start.1 = (bf16[256,768]{0,1:T(8,128)(2,1)S(1)}, bf16[256,768]{0,1:T(8,128)(2,1)S(1)}, u32[]{:S(2)}, u32[]{:S(2)}) collective-permute-start(bf16[256,768]{0,1:T(8,128)(2,1)S(1)} %fusion.15), channel_id=1, source_target_pairs={{8,0},{16,8},{24,16},{32,24},{40,32},{48,40},{56,48},{64,56},{72,6... | collective-permute-start | bytes 1179656 | tf_op jit(solution)/shard_map/ppermute | solution.py:23
  57.2 1.0 %copy-start.3 = (bf16[1,256,768]{1,2,0:T(8,128)(2,1)S(1)}, bf16[1,256,768]{1,2,0:T(8,128)(2,1)}, u32[]{:S(2)}) copy-start(bf16[1,256,768]{1,2,0:T(8,128)(2,1)} %copy-done.2) | copy-start | bytes 1179652
  58.2 1.9 %copy-start.5 = (f32[6,256,256]{1,2,0:T(8,128)S(1)}, f32[6,256,256]{1,2,0:T(8,128)}, u32[]{:S(2)}) copy-start(f32[6,256,256]{1,2,0:T(8,128)} %copy-done.4) | copy-start | bytes 4718596
  62.0 1.1 %copy-start.11 = (f32[6,256]{0,1:T(8,128)S(1)}, f32[6,256]{0,1:T(8,128)}, u32[]{:S(2)}) copy-start(f32[6,256]{0,1:T(8,128)} %copy.121) | copy-start | bytes 18436
  62.9 1.0 %copy-start.8 = (bf16[256,768]{0,1:T(8,128)(2,1)S(1)}, bf16[256,768]{0,1:T(8,128)(2,1)}, u32[]{:S(2)}) copy-start(bf16[256,768]{0,1:T(8,128)(2,1)} %copy-done.7) | copy-start | bytes 1179652
  62.9 1.0 %copy-start.14 = (f32[6,256]{1,0:T(8,128)S(1)}, f32[6,256]{1,0:T(8,128)}, u32[]{:S(2)}) copy-start(f32[6,256]{1,0:T(8,128)} %get-tuple-element.22) | copy-start | bytes 18436
  63.0 1.4 %copy-start.6 = (f32[6,256,256]{1,2,0:T(8,128)S(1)}, f32[6,256,256]{1,2,0:T(8,128)}, u32[]{:S(2)}) copy-start(f32[6,256,256]{1,2,0:T(8,128)} %get-tuple-element.23) | copy-start | bytes 4718596
  65.5 1.0 %copy-start = (bf16[1,256,768]{2,1,0:T(8,128)(2,1)S(1)}, bf16[1,256,768]{2,1,0:T(8,128)(2,1)}, u32[]{:S(2)}) copy-start(bf16[1,256,768]{2,1,0:T(8,128)(2,1)} %copy.132) | copy-start | bytes 1179652
  65.5 1.1 %copy-start.1 = (bf16[1,256,768]{2,1,0:T(8,128)(2,1)S(1)}, bf16[1,256,768]{2,1,0:T(8,128)(2,1)}, u32[]{:S(2)}) copy-start(bf16[1,256,768]{2,1,0:T(8,128)(2,1)} %copy.126) | copy-start | bytes 1179652
